TPU v7x, 32 devices: a whole 2x2x4 slice. The times are simulated.
32 devices in a mesh: row: 8 (over z, core), col: 4 (over y, x).
Axes of the slice: x: 2, y: 2, z: 4, core: 2. Of those that a mesh axis runs over, the one named last changes fastest.
Arguments:
- features: bfloat16 [9, 1, 128, 128, 128], P(None, None, 'row', 'col'), may hold values from -12 to 12
- cotangent: float32 [3, 1, 128, 128, 128], P(None, None, 'row', 'col'), may hold values from -14 to 14
- w_in: bfloat16 [9, 256], replicated, may hold values from -2 to 2
- bias_in: float32 [256], replicated, may hold values from -3 to 3
- w_mid: bfloat16 [256, 256], replicated, may hold values from -0.375 to 0.375
- bias_mid: float32 [256], replicated, may hold values from -3 to 3
- w_out: bfloat16 [256, 6], replicated, may hold values from -2.5 to 2.5
Outputs:
- grad_features: float32 [9, 1, 128, 128, 128], P(None, None, 'row', 'col')
- grad_w_in: float32 [9, 256], replicated
- grad_b_in: float32 [256], replicated
- grad_w_mid: float32 [256, 256], replicated
- grad_b_mid: float32 [256], replicated
- grad_w_out: float32 [256, 6], replicated
All inputs are finite; a program needn't handle non-finite values.
Results may differ from a plain program's by a relative error of at most 0.025.
Values sent between devices are 32-bit elements; how exact they have to be, the bound alone decides.
A program may use at most 128 MiB of HBM per device.

v0:
```python
import math
import jax
import jax.numpy as jnp
from jax import lax
from jax.sharding import PartitionSpec as P

NX = 128
NY = 128
NZ = 128
CELLS = 2097152
STEP_DT = 0.04
PAIRS = ((0, 0), (1, 1), (2, 2), (0, 1), (0, 2), (1, 2))


def mode_list(count, length):
    index = jnp.arange(count, dtype=jnp.int32)
    return jnp.where(index < length // 2, index, index - length)


def phase_table(modes, length):
    positions = jnp.arange(length, dtype=jnp.int32)
    turns = positions[:, None] * modes[None, :] % length
    angle = turns.astype(jnp.float32) * (2.0 * math.pi / length)
    return (jnp.cos(angle), jnp.sin(angle))


def contract(form, left, right):
    return jnp.einsum(
        form, left, right, precision=lax.Precision.HIGHEST, preferred_element_type=jnp.float32
    )


def complex_product(form, part, table_real, table_imag):
    real = contract(form, part[0], table_real) - contract(form, part[1], table_imag)
    imag = contract(form, part[0], table_imag) + contract(form, part[1], table_real)
    return jnp.stack([real, imag])


def closure_block(x_blk, g_blk, w_in, bias_in, w_mid, bias_mid, w_out):
    pre_in = (
        jnp.einsum("fh,fn->hn", w_in, x_blk, preferred_element_type=jnp.float32) + bias_in[:, None]
    )
    act_in = jnp.tanh(pre_in).astype(jnp.bfloat16)
    pre_mid = (
        jnp.einsum("io,in->on", w_mid, act_in, preferred_element_type=jnp.float32)
        + bias_mid[:, None]
    )
    act_mid = jnp.tanh(pre_mid).astype(jnp.bfloat16)
    back_mid = jnp.einsum("ho,on->hn", w_out, g_blk, preferred_element_type=jnp.float32)
    delta_mid = (back_mid * (1.0 - jnp.square(act_mid.astype(jnp.float32)))).astype(jnp.bfloat16)
    back_in = jnp.einsum("io,on->in", w_mid, delta_mid, preferred_element_type=jnp.float32)
    delta_in = (back_in * (1.0 - jnp.square(act_in.astype(jnp.float32)))).astype(jnp.bfloat16)
    grad_x = jnp.einsum("fh,hn->fn", w_in, delta_in, preferred_element_type=jnp.float32)
    gw_out = jnp.einsum("hn,on->ho", act_mid, g_blk, preferred_element_type=jnp.float32)
    gw_mid = jnp.einsum("in,on->io", act_in, delta_mid, preferred_element_type=jnp.float32)
    gw_in = jnp.einsum("fn,hn->fh", x_blk, delta_in, preferred_element_type=jnp.float32)
    gb_mid = jnp.sum(delta_mid.astype(jnp.float32), axis=1)
    gb_in = jnp.sum(delta_in.astype(jnp.float32), axis=1)
    return (grad_x, (gw_in, gb_in, gw_mid, gb_mid, gw_out))


def per_device(features, cotangent, w_in, bias_in, w_mid, bias_mid, w_out):
    rows_group = lax.axis_size("row")
    cols_group = lax.axis_size("col")
    count_y = NY
    count_z = NZ
    list_z = mode_list(count_z, NZ)
    weight_z = jnp.ones((count_z,), jnp.float32) / NZ
    list_x = mode_list(NX, NX)
    list_y = mode_list(count_y, NY)
    cos_x, sin_x = phase_table(list_x, NX)
    cos_y, sin_y = phase_table(list_y, NY)
    cos_z, sin_z = phase_table(list_z, NZ)
    forward_z = jnp.stack(
        [
            contract("csxyz,zk->csxky", cotangent, cos_z),
            -contract("csxyz,zk->csxky", cotangent, sin_z),
        ]
    )
    spectra = complex_product(
        "csxky,yq->cskqx",
        lax.all_to_all(forward_z, "col", split_axis=4, concat_axis=5, tiled=True),
        cos_y,
        -sin_y,
    )
    spectra = complex_product(
        "cskqx,xp->cskqp",
        lax.all_to_all(spectra, "row", split_axis=4, concat_axis=5, tiled=True),
        cos_x,
        -sin_x,
    )
    share_y = count_y // rows_group
    share_z = count_z // cols_group
    local_y = lax.dynamic_slice_in_dim(list_y, lax.axis_index("row") * share_y, share_y)
    local_z = lax.dynamic_slice_in_dim(list_z, lax.axis_index("col") * share_z, share_z)
    modes_x = list_x[None, None, :]
    modes_y = local_y[None, :, None]
    modes_z = local_z[:, None, None]
    keep = (3 * jnp.abs(modes_x) < NX) & (3 * jnp.abs(modes_y) < NY) & (3 * jnp.abs(modes_z) < NZ)
    waves = [modes_x.astype(jnp.float32), modes_y.astype(jnp.float32), modes_z.astype(jnp.float32)]
    velocity = [spectra[:, comp] for comp in range(3)]
    inner = waves[0] * velocity[0] + waves[1] * velocity[1] + waves[2] * velocity[2]
    square = jnp.maximum(waves[0] * waves[0] + waves[1] * waves[1] + waves[2] * waves[2], 1.0)
    projected = [
        jnp.where(keep, velocity[comp] - waves[comp] * inner / square, 0.0) for comp in range(3)
    ]
    stress_parts = []
    for first, second in PAIRS:
        if first == second:
            value = waves[first] * projected[first]
        else:
            value = waves[second] * projected[first] + waves[first] * projected[second]
        stress_parts.append(jnp.stack([-STEP_DT * value[1], STEP_DT * value[0]]))
    stress_hat = jnp.stack(stress_parts, axis=1)
    back_x = complex_product("cskqp,px->cskxq", stress_hat, cos_x.T / NX, sin_x.T / NX)
    stress_mid = complex_product(
        "cskxq,qy->csxyk",
        lax.all_to_all(back_x, "row", split_axis=4, concat_axis=5, tiled=True),
        cos_y.T / NY,
        sin_y.T / NY,
    )
    real_z = cos_z.T * weight_z[:, None]
    imag_z = sin_z.T * weight_z[:, None]
    part = lax.all_to_all(stress_mid, "col", split_axis=4, concat_axis=5, tiled=True)
    stress = contract("csxyk,kz->csxyz", part[0], real_z) - contract(
        "csxyk,kz->csxyz", part[1], imag_z
    )
    inputs_count = features.shape[0]
    stress_count = stress.shape[0]
    cells = stress.shape[1] * stress.shape[2] * stress.shape[3] * stress.shape[4]
    feats = features.reshape(inputs_count, cells)
    grads = stress.astype(jnp.bfloat16).reshape(stress_count, cells)
    hidden = w_mid.shape[0]
    blank = jnp.zeros((inputs_count, cells), jnp.float32)
    block = math.gcd(cells, max(1024, cells // 8))

    def visit(index, carry):
        current, totals = carry
        start = (0 + index * block).astype(jnp.int32)
        x_blk = lax.dynamic_slice_in_dim(feats, start, block, 1)
        g_blk = lax.dynamic_slice_in_dim(grads, start, block, 1)
        grad_x, parts = closure_block(x_blk, g_blk, w_in, bias_in, w_mid, bias_mid, w_out)
        current = lax.dynamic_update_slice_in_dim(current, grad_x, start, 1)
        return (current, tuple((a + b for a, b in zip(totals, parts))))

    init = (
        jnp.zeros((inputs_count, hidden), jnp.float32),
        jnp.zeros((hidden,), jnp.float32),
        jnp.zeros((hidden, hidden), jnp.float32),
        jnp.zeros((hidden,), jnp.float32),
        jnp.zeros((hidden, stress_count), jnp.float32),
    )
    field, local = lax.fori_loop(0, cells // block, visit, (blank, init))
    totals = lax.psum((local[0], local[1], local[2], local[3], local[4]), ("row", "col"))
    factor = 1.0 / math.sqrt(CELLS)
    return (
        field.reshape(features.shape),
        totals[0] * factor,
        totals[1] * factor,
        totals[2] * factor,
        totals[3] * factor,
        totals[4] * factor,
    )


def solution(mesh):
    return jax.shard_map(
        per_device,
        mesh=mesh,
        in_specs=(
            P(None, None, "row", "col", None),
            P(None, None, "row", "col", None),
            P(),
            P(),
            P(),
            P(),
            P(),
        ),
        out_specs=(P(None, None, "row", "col", None), P(), P(), P(), P(), P()),
        check_vma=False,
    )
```

profile of v0, /device:TPU:0, one launch (start us, length us, event | category | flops | bytes accessed | tf_op | source)
XLA Modules:
  0.0 856.4 jit_solution(18035341283685795229)
XLA Ops:
  10.6 6.0 copy.51
  16.6 5.9 reshape.562
  22.5 25.4 %all_to_all.60 = f32[4,1,98304]{2,1,0:T(1,128)S(1)} all-to-all(f32[4,1,98304]{2,1,0:T(1,128)} %reshape.562), channel_id=1, replica_groups=mesh['row'=8,'col'=4] {'col'}, dimensions={0} | all-to-all | bytes 3145728 | tf_op jit(solution)/shard_map/all_to_all | solution.py:82
  48.4 6.4 reduce.2
  54.7 6.3 reshape.563
  61.0 6.8 copy.95
  81.1 6.0 copy.53
  87.1 7.6 reshape.564
  94.7 5.2 all-to-all-start.1
  100.6 36.9 %all-to-all-done.1 = f32[8,1,49152]{2,1,0:T(1,128)S(1)} async-done(((f32[8,1,49152]{2,1,0:T(1,128)}), f32[8,1,49152]{2,1,0:T(1,128)S(1)}, u32[]{:S(2)}, u32[]{:S(2)}) %all-to-all-start.1) | async-done | bytes 1572896 | tf_op jit(solution)/shard_map/all_to_all | solution.py:88
  137.5 6.2 reduce.3
  143.7 6.1 reshape.565
  154.4 5.1 fusion.55
  159.5 5.5 fusion.48
  165.4 5.1 fusion.21
  170.5 5.1 fusion.20
  186.4 11.4 %copy.63 = f32[2,6,1,32,128,16]{3,5,1,2,0,4:T(8,128)} copy(f32[2,6,1,32,128,16]{4,3,5,1,2,0:T(8,128)} %pad_maximum_fusion) | data formatting | bytes 6291456 | tf_op jit(solution)/shard_map/stack | solution.py:36
  197.8 10.6 %reshape.566 = f32[8,1,98304]{2,1,0:T(1,128)} reshape(f32[128,2,1,6,16,32]{5,4,3,2,1,0:T(8,128)} %bitcast.283) | data formatting | bytes 6291456
  208.5 76.0 %all_to_all.61 = f32[8,1,98304]{2,1,0:T(1,128)} all-to-all(f32[8,1,98304]{2,1,0:T(1,128)} %reshape.566), channel_id=1, replica_groups=mesh['row'=8,'col'=4] {'row'}, dimensions={0} | all-to-all | bytes 6291456 | tf_op jit(solution)/shard_map/all_to_all | solution.py:118
  284.4 11.7 %reduce.4 = f32[8,98304]{1,0:T(8,128)} reduce(f32[8,1,98304]{2,1,0:T(1,128)} %all_to_all.61, f32[]{:T(128)} %broadcast.808), dimensions={1}, to_apply=%all_to_all.50.reduce_sub_computation | reduce | bytes 6291460 | tf_op jit(solution)/shard_map/all_to_all | solution.py:118
  296.1 10.9 %reshape.567 = f32[128,2,1,6,16,32]{5,4,3,2,1,0:T(8,128)} reshape(f32[8,98304]{1,0:T(8,128)} %reduce.4) | data formatting | bytes 6291456
  307.0 10.4 %copy.64 = f32[2,6,1,32,128,16]{3,5,4,1,0,2:T(8,128)} copy(f32[2,6,1,32,128,16]{3,5,1,2,0,4:T(8,128)} %bitcast.281) | data formatting | bytes 6291456 | tf_op jit(solution)/shard_map/all_to_all | solution.py:118
  317.4 10.7 %fusion.205 = (f32[1,6,1,32,16,8,16]{3,6,4,5,1,0,2:T(8,128)}, f32[1,6,1,32,16,8,16]{3,6,4,5,1,0,2:T(8,128)}) fusion(f32[2,6,1,32,16,8,16]{3,6,4,5,1,0,2:T(8,128)} %bitcast.279), kind=kLoop, calls=%fused_computation.273 | loop fusion | bytes 6291456 | tf_op jit(solution)/shard_map/slice | solution.py:34
  328.1 3.7 copy.65
  331.8 10.1 %fusion.64 = f32[128,6,32,16]{0,2,3,1:T(8,128)S(1)} fusion(f32[6,32,16,128]{1,3,2,0:T(8,128)S(1)} %bitcast.277, s32[128]{0:T(128)S(1)} %compare_select_fusion), kind=kOutput, calls=%fused_computation.138 | convolution fusion | flops 604225536 | bytes 3146240 | tf_op jit(solution)/shard_map/cskxq,qy->csxyk/dot_general | solution.py:28
  341.9 10.2 %fusion.43 = f32[128,6,32,16]{0,2,3,1:T(8,128)S(1)} fusion(f32[6,32,16,128]{1,3,2,0:T(8,128)S(1)} %bitcast.278, s32[128]{0:T(128)S(1)} %compare_select_fusion), kind=kOutput, calls=%fused_computation.117 | convolution fusion | flops 604225536 | bytes 3146240 | tf_op jit(solution)/shard_map/cskxq,qy->csxyk/dot_general | solution.py:28
  353.1 10.5 %subtract_bitcast_fusion = f32[1,6,1,16,128,32]{4,5,3,1,2,0:T(8,128)S(1)} fusion(f32[128,6,32,16]{0,2,3,1:T(8,128)S(1)} %fusion.64, f32[6,32,16,128]{1,3,2,0:T(8,128)S(1)} %bitcast.275, s32[128]{0:T(128)S(1)} %compare_select_fusion), kind=kOutput, calls=%fused_computation.41 | convolution fusion | flops 604618752 | bytes 4719104 | tf_op jit(solution)/shard_map/cskxq,qy->csxyk/dot_general | solution.py:28
  363.6 10.1 %add_bitcast_fusion = f32[1,6,1,16,128,32]{4,5,3,1,2,0:T(8,128)S(1)} fusion(f32[128,6,32,16]{0,2,3,1:T(8,128)S(1)} %fusion.43, f32[6,32,16,128]{1,3,2,0:T(8,128)S(1)} %bitcast.276, s32[128]{0:T(128)S(1)} %compare_select_fusion), kind=kOutput, calls=%fused_computation.40 | convolution fusion | flops 604618752 | bytes 4719104 | tf_op jit(solution)/shard_map/cskxq,qy->csxyk/dot_general | solution.py:28
  375.7 11.4 %copy.71 = f32[2,6,1,16,128,32]{5,3,1,2,0,4:T(8,128)} copy(f32[2,6,1,16,128,32]{4,5,3,1,2,0:T(8,128)} %pad_maximum_fusion.1) | data formatting | bytes 6291456 | tf_op jit(solution)/shard_map/stack | solution.py:36
  387.1 9.3 %reshape.568 = f32[4,1,196608]{2,1,0:T(1,128)} reshape(f32[128,2,1,6,16,32]{5,4,3,2,1,0:T(8,128)} %bitcast.284) | data formatting | bytes 6291456
  396.4 4.8 all-to-all-start.3
  404.2 33.1 %all-to-all-done.3 = f32[4,1,196608]{2,1,0:T(1,128)} async-done(((f32[4,1,196608]{2,1,0:T(1,128)}), f32[4,1,196608]{2,1,0:T(1,128)}, u32[]{:S(2)}, u32[]{:S(2)}) %all-to-all-start.3) | async-done | bytes 3145760 | tf_op jit(solution)/shard_map/all_to_all | solution.py:124
  437.3 11.8 %reduce.5 = f32[4,196608]{1,0:T(4,128)} reduce(f32[4,1,196608]{2,1,0:T(1,128)} %all-to-all-done.3, f32[]{:T(128)} %broadcast.808), dimensions={1}, to_apply=%all_to_all.53.reduce_sub_computation | reduce | bytes 6291460 | tf_op jit(solution)/shard_map/all_to_all | solution.py:124
  449.1 10.7 %reshape.569 = f32[128,2,1,6,16,32]{5,4,3,2,1,0:T(8,128)} reshape(f32[4,196608]{1,0:T(4,128)} %reduce.5) | data formatting | bytes 6291456
  459.9 16.4 %copy.94 = f32[2,6,1,16,4,32,32]{6,4,5,3,1,2,0:T(4,128)} copy(f32[2,6,1,16,4,32,32]{6,3,1,0,5,4,2:T(8,128)} %bitcast.282) | data formatting | bytes 6291456 | tf_op jit(solution)/shard_map/all_to_all | solution.py:124
  476.3 14.3 %fusion.204 = (f32[1,6,1,16,32,4,32]{6,5,4,3,1,2,0:T(4,128)}, f32[1,6,1,16,32,4,32]{6,5,4,3,1,2,0:T(4,128)}) fusion(f32[2,6,1,16,32,4,32]{6,5,4,3,1,2,0:T(4,128)} %bitcast.280), kind=kLoop, calls=%fused_computation.272 | loop fusion | bytes 6291456 | tf_op jit(solution)/shard_map/slice | solution.py:126
  490.7 6.0 reshape.552
  499.7 5.8 reshape.553
  511.5 165.8 %while.24 = (s32[]{:T(128)}, f32[9,65536]{1,0:T(8,128)}, f32[9,256]{1,0:T(8,128)S(1)}, f32[256]{0:T(256)S(1)}, f32[256,256]{1,0:T(8,128)S(1)}, /*index=5*/f32[25...) while((s32[]{:T(128)}, f32[9,65536]{1,0:T(8,128)}, ...), condition=%wide.region_3.4_spmd.clone, body=%wide.region_0.3_spmd.clone.sunk | while | flops 3422691328 | bytes 157343136 | solution.py:153
  517.5 3.9 convert_reduce_fusion.5
  521.4 4.3 fusion.269
  538.2 3.9 convert_reduce_fusion.5
  542.1 4.4 fusion.269
  546.5 3.7 convolution_add_fusion.11
  558.9 3.9 convert_reduce_fusion.5
  562.8 4.4 fusion.269
  567.2 3.7 convolution_add_fusion.11
  579.6 3.9 convert_reduce_fusion.5
  583.5 4.3 fusion.269
  587.9 3.7 convolution_add_fusion.11
  600.2 3.9 convert_reduce_fusion.5
  604.2 4.4 fusion.269
  608.6 3.7 convolution_add_fusion.11
  621.0 3.9 convert_reduce_fusion.5
  624.9 4.4 fusion.269
  629.3 3.7 convolution_add_fusion.11
  641.6 3.9 convert_reduce_fusion.5
  645.6 4.3 fusion.269
  650.0 3.7 convolution_add_fusion.11
  662.3 3.9 convert_reduce_fusion.5
  666.3 4.3 fusion.269
  670.6 3.7 convolution_add_fusion.11
  677.3 37.5 %all-reduce = (f32[9,256]{1,0:T(8,128)S(1)}, f32[256]{0:T(256)S(1)}, f32[256]{0:T(256)S(1)}, f32[256,6]{0,1:T(8,128)S(1)}) all-reduce(f32[9,256]{1,0:T(8,128)S(1)} %get-tuple-element.241, f32[256]{0:T(256)S(1)} %get-tuple-element.242, f32[256]{0:T(256)S(1)} %get-tuple-element.244, ...), channel_id=1, replica_groups=mesh['row'=8,'col'=4] {'row','col'}, use_global_device_ids=true, to_apply=%region_4.5 | all-reduce | flops 4352 | bytes 34816 | tf_op jit(solution)/shard_map/psum | solution.py:154
  721.8 125.8 %all-reduce.3.cloned.1.call-done = f32[256,256]{1,0:T(8,128)} async-done(((f32[256,256]{1,0:T(8,128)}), f32[256,256]{1,0:T(8,128)}) %all-reduce.3.cloned.1.call-update) | async-done | bytes 262160 | tf_op jit(solution)/shard_map/psum | solution.py:154
  (236 shorter events, 129.4 us)
Async XLA Ops:
  7.2 1.1 copy-start
  94.7 42.8 %all-to-all-start.1 = ((f32[8,1,49152]{2,1,0:T(1,128)}), f32[8,1,49152]{2,1,0:T(1,128)S(1)}, u32[]{:S(2)}, u32[]{:S(2)}) async-start(f32[8,1,49152]{2,1,0:T(1,128)} %reshape.564), calls=%async_computation.1 | async-start | bytes 3145728 | tf_op jit(solution)/shard_map/all_to_all | solution.py:88
  331.8 20.3 %slice-start = ((s8[6291456]{0:T(1024)(128)(4,1)}), s8[4194304]{0:T(1024)(128)(4,1)S(1)}, s32[]{:S(2)}) async-start(s8[6291456]{0:T(1024)(128)(4,1)} %bitcast.291), calls=%async_computation.5 | async-start | bytes 8388608
  341.9 10.3 %slice-start.1 = ((s8[6291456]{0:T(1024)(128)(4,1)}), s8[2097152]{0:T(1024)(128)(4,1)S(1)}, s32[]{:S(2)}) async-start(s8[6291456]{0:T(1024)(128)(4,1)} %bitcast.291), calls=%async_computation.6 | async-start | bytes 4194304
  396.4 4.9 copy-start.9
  396.4 40.9 %all-to-all-start.3 = ((f32[4,1,196608]{2,1,0:T(1,128)}), f32[4,1,196608]{2,1,0:T(1,128)}, u32[]{:S(2)}, u32[]{:S(2)}) async-start(f32[4,1,196608]{2,1,0:T(1,128)} %reshape.568), calls=%async_computation.3 | async-start | bytes 6291456 | tf_op jit(solution)/shard_map/all_to_all | solution.py:124
  401.2 446.4 %all-reduce.3.cloned.1.call-start = ((), (), s32[]{:S(2)}) async-start(), calls=%async_computation.4 | async-start | bytes 524288 | tf_op jit(solution)/shard_map/psum | solution.py:154
  508.6 2.8 copy-start.10
  508.7 2.8 copy-start.11
  508.7 2.8 copy-start.12
  508.7 2.8 copy-start.13
  508.7 2.8 copy-start.14
  514.1 3.4 copy-start.3
  515.4 2.1 copy-start.6
  517.5 4.0 copy-start.5
  521.4 4.4 copy-start.4
  525.8 3.7 copy-start.2
  529.5 2.3 copy-start.7
  534.8 3.4 copy-start.3
  536.1 2.1 copy-start.6
  538.2 4.0 copy-start.5
  542.1 4.4 copy-start.4
  546.5 3.7 copy-start.2
  550.2 2.3 copy-start.7
  555.5 3.4 copy-start.3
  556.8 2.1 copy-start.6
  558.8 4.0 copy-start.5
  562.8 4.4 copy-start.4
  567.2 3.7 copy-start.2
  570.9 2.3 copy-start.7
  576.2 3.4 copy-start.3
  577.5 2.1 copy-start.6
  579.5 4.0 copy-start.5
  583.5 4.4 copy-start.4
  587.9 3.7 copy-start.2
  591.6 2.3 copy-start.7
  596.9 3.4 copy-start.3
  598.1 2.1 copy-start.6
  600.2 4.0 copy-start.5
  604.2 4.4 copy-start.4
  608.6 3.7 copy-start.2
  612.3 2.3 copy-start.7
  617.6 3.4 copy-start.3
  618.9 2.1 copy-start.6
  620.9 4.0 copy-start.5
  624.9 4.4 copy-start.4
  629.3 3.7 copy-start.2
  633.0 2.3 copy-start.7
  638.3 3.3 copy-start.3
  639.6 2.1 copy-start.6
  641.6 4.0 copy-start.5
  645.6 4.4 copy-start.4
  650.0 3.7 copy-start.2
  653.7 2.3 copy-start.7
  659.0 3.4 copy-start.3
  660.2 2.1 copy-start.6
  662.3 4.0 copy-start.5
  666.3 4.3 copy-start.4
  670.6 3.7 copy-start.2
  674.3 2.3 copy-start.7
  677.3 42.4 %copy-start.8 = (f32[256,256]{1,0:T(8,128)}, f32[256,256]{1,0:T(8,128)S(1)}, u32[]{:S(2)}) copy-start(f32[256,256]{1,0:T(8,128)S(1)} %get-tuple-element.243) | copy-start | bytes 786436
  716.5 132.8 %copy-start.1 = (f32[3,1,16,32,128]{4,3,2,1,0:T(8,128)S(1)}, f32[3,1,16,32,128]{4,3,2,1,0:T(8,128)}, u32[]{:S(2)}) copy-start(f32[3,1,16,32,128]{4,3,2,1,0:T(8,128)} %param.10) | copy-start | bytes 2359300
Sparse Core Ops, SparseCore 0:
  721.3 126.2 all-reduce.2
where the time goes:
time: 862 us; the launch traced here: 856 us
  matrix products  242 us (28%)
  local copies, waits for them, and re-layouts  207 us (24%)
  waiting for transfers between devices  196 us (23%)
  blocking collectives  139 us (16%)
  other arithmetic  46.9 us (5%)
  between operations  14.9 us (2%)
  starting transfers between devices  9.97 us (1%)
    psum x1, waiting for transfers between devices, per_device(): lax.psum((local[0], local[1], local[2], local[3], local[4]), ('row', 'col'))  126 us
    dot_general x20, matrix products, contract(): jnp.einsum(form, left, right, precision=lax.Precision.HIGHEST, preferred_...  81.1 us
    unnamed x35, local copies, waits for them, and re-layouts  76.7 us
    all_to_all x1, blocking collectives, per_device(): lax.all_to_all(back_x, 'row', split_axis=4, concat_axis=5, tiled=True)  76 us
    psum x1, blocking collectives, per_device(): lax.psum((local[0], local[1], local[2], local[3], local[4]), ('row', 'col'))  37.5 us
    all_to_all x1, waiting for transfers between devices, per_device(): lax.all_to_all(spectra, 'row', split_axis=4, concat_axis=5, tiled=True)  36.9 us
    dot_general x8, matrix products, closure_block(): jnp.einsum('fh,hn->fn', w_in, delta_in, preferred_element_type=jnp.float32)  34.8 us
    all_to_all x1, waiting for transfers between devices, per_device(): lax.all_to_all(stress_mid, 'col', split_axis=4, concat_axis=5, tiled=True)  33.1 us
  transfers between devices with their start and end apart: 3, of which 3 were waited for; matrix products, arithmetic and copies ran while one was open for 0% of the time, Pallas kernels for 0%

commit v1 on v0

--- a/solution.py
+++ b/solution.py
@@ -10,6 +10,22 @@
 CELLS = 2097152
 STEP_DT = 0.04
 PAIRS = ((0, 0), (1, 1), (2, 2), (0, 1), (0, 2), (1, 2))
+
+
+def swapped_with_each(shard, axis, split, join):
+    ways, here = (lax.axis_size(axis), lax.axis_index(axis))
+    width = shard.shape[split] // ways
+    lengths = list(shard.shape)
+    lengths[split] = width
+    height = lengths[join]
+    lengths[join] = height * ways
+    full = jnp.zeros(lengths, shard.dtype)
+    for mask in range(ways):
+        part = lax.dynamic_slice_in_dim(shard, (here ^ mask) * width, width, axis=split)
+        if mask:
+            part = lax.ppermute(part, axis, [(d, d ^ mask) for d in range(ways)])
+        full = lax.dynamic_update_slice_in_dim(full, part, (here ^ mask) * height, axis=join)
+    return full
 
 
 def mode_list(count, length):
@@ -114,10 +130,7 @@
     stress_hat = jnp.stack(stress_parts, axis=1)
     back_x = complex_product("cskqp,px->cskxq", stress_hat, cos_x.T / NX, sin_x.T / NX)
     stress_mid = complex_product(
-        "cskxq,qy->csxyk",
-        lax.all_to_all(back_x, "row", split_axis=4, concat_axis=5, tiled=True),
-        cos_y.T / NY,
-        sin_y.T / NY,
+        "cskxq,qy->csxyk", swapped_with_each(back_x, "row", 4, 5), cos_y.T / NY, sin_y.T / NY
     )
     real_z = cos_z.T * weight_z[:, None]
     imag_z = sin_z.T * weight_z[:, None]

time: 862 us -> 1070 us (1.24)
  local copies, waits for them, and re-layouts: 207 us -> 455 us
  blocking collectives: 139 us -> 62.5 us
  waiting for transfers between devices: 196 us -> 257 us
  matrix products: 242 us -> 209 us
    dynamic_update_slice x0 -> x8, local copies, waits for them, and re-layouts: none -> 254 us  [swapped_with_each(): lax.dynamic_update_slice_in_dim(full, part, (here ^ mask) * height, axis=...]
    all_to_all x1 -> x0, blocking collectives: 76 us -> none  [per_device(): lax.all_to_all(back_x, 'row', split_axis=4, concat_axis=5, tiled=True)]
    ppermute x0 -> x7, waiting for transfers between devices: none -> 59.5 us  [swapped_with_each(): part = lax.ppermute(part, axis, [(d, d ^ mask) for d in range(ways)])]
    dot_general x20, matrix products: 81.1 us -> 48.8 us  [contract(): jnp.einsum(form, left, right, precision=lax.Precision.HIGHEST, preferred_...]
    dynamic_slice x0 -> x8, local copies, waits for them, and re-layouts: none -> 27.4 us  [swapped_with_each(): lax.dynamic_slice_in_dim(shard, (here ^ mask) * width, width, axis=split)]
    ppermute x0 -> x7, local copies, waits for them, and re-layouts: none -> 23 us  [swapped_with_each(): part = lax.ppermute(part, axis, [(d, d ^ mask) for d in range(ways)])]
    unnamed x35 -> x33, local copies, waits for them, and re-layouts: 76.7 us -> 55.2 us
    another operation x3 -> x4, other arithmetic: 4.14 us -> 18.2 us  [complex_product(): return jnp.stack([real, imag])]
  transfers between devices with their start and end apart: 3 -> 10, of which waited for: 3 -> 4; matrix products, arithmetic and copies ran while one was open for 0% -> 26% of each run, Pallas kernels for 0% -> 0%
where the time goes in v1:
time: 1070 us
  local copies, waits for them, and re-layouts  455 us (43%)
  waiting for transfers between devices  257 us (24%)
  matrix products  209 us (20%)
  blocking collectives  62.5 us (6%)
  other arithmetic  49.2 us (5%)
  starting transfers between devices  17.1 us (2%)
  between operations  15 us (1%)
    dynamic_update_slice x8, local copies, waits for them, and re-layouts, swapped_with_each(): lax.dynamic_update_slice_in_dim(full, part, (here ^ mask) * height, axis=...  254 us
    psum x1, waiting for transfers between devices, per_device(): lax.psum((local[0], local[1], local[2], local[3], local[4]), ('row', 'col'))  126 us
    ppermute x7, waiting for transfers between devices, swapped_with_each(): part = lax.ppermute(part, axis, [(d, d ^ mask) for d in range(ways)])  59.5 us
    unnamed x33, local copies, waits for them, and re-layouts  55.2 us
    dot_general x20, matrix products, contract(): jnp.einsum(form, left, right, precision=lax.Precision.HIGHEST, preferred_...  48.8 us
    psum x1, blocking collectives, per_device(): lax.psum((local[0], local[1], local[2], local[3], local[4]), ('row', 'col'))  37.1 us
    all_to_all x1, waiting for transfers between devices, per_device(): lax.all_to_all(spectra, 'row', split_axis=4, concat_axis=5, tiled=True)  36.9 us
    dot_general x8, matrix products, closure_block(): jnp.einsum('fh,hn->fn', w_in, delta_in, preferred_element_type=jnp.float32)  34.8 us
  transfers between devices with their start and end apart: 10, of which 4 were waited for; matrix products, arithmetic and copies ran while one was open for 26% of the time, Pallas kernels for 0%

profile of v1, /device:TPU:0, one launch (start us, length us, event | category | flops | bytes accessed | tf_op | source)
XLA Modules:
  0.0 1065.7 jit_solution(1423638632013207820)
XLA Ops:
  10.6 6.0 copy.58
  16.6 5.9 reshape.558
  22.5 25.4 %all_to_all.45 = f32[4,1,98304]{2,1,0:T(1,128)S(1)} all-to-all(f32[4,1,98304]{2,1,0:T(1,128)} %reshape.558), channel_id=1, replica_groups=mesh['row'=8,'col'=4] {'col'}, dimensions={0} | all-to-all | bytes 3145728 | tf_op jit(solution)/shard_map/all_to_all | solution.py:98
  48.4 6.4 reduce.2
  54.8 6.2 reshape.559
  61.0 6.8 copy.105
  81.1 6.0 copy.60
  87.1 7.6 reshape.560
  94.8 5.2 all-to-all-start.1
  100.7 36.9 %all-to-all-done.1 = f32[8,1,49152]{2,1,0:T(1,128)S(1)} async-done(((f32[8,1,49152]{2,1,0:T(1,128)}), f32[8,1,49152]{2,1,0:T(1,128)S(1)}, u32[]{:S(2)}, u32[]{:S(2)}) %all-to-all-start.1) | async-done | bytes 1572896 | tf_op jit(solution)/shard_map/all_to_all | solution.py:104
  137.6 6.2 reduce.3
  143.7 6.1 reshape.561
  154.4 5.1 fusion.64
  159.5 5.5 fusion.57
  165.4 5.1 fusion.31
  170.5 5.1 fusion.30
  184.4 9.9 fusion.15
  201.1 6.2 fusion.22
  228.4 59.5 %collective-permute-done.1 = f32[2,6,1,32,16,16]{3,5,4,2,1,0:T(8,128)} collective-permute-done((f32[2,6,1,32,16,16]{3,5,4,2,1,0:T(8,128)}, f32[2,6,1,32,16,16]{3,5,4,2,1,0:T(8,128)}, u32[]{:S(2)}, u32[]{:S(2)}) %collective-permute-start.1) | collective-permute-done | bytes 393248 | tf_op jit(solution)/shard_map/ppermute | solution.py:26
  289.3 5.2 copy.70
  296.6 16.0 %dynamic_update_slice.31 = f32[2,6,1,32,16,128]{5,3,4,1,2,0:T(8,128)} dynamic-update-slice(f32[2,6,1,32,16,128]{5,3,4,1,2,0:T(8,128)} %broadcast_in_dim.30, f32[2,6,1,32,16,16]{5,3,4,1,2,0:T(8,128)} %copy.70, s32[]{:T(128)} %constant.104.clone.1, s32[]{:T(128)} %constant.104.clone.1, s32[]{:T(128)} %constant.104.clone.1, s32[]{:T(128)} %constant.104.clone.1, s32[]{:T(128)} %constant.104.clone.1, ...) | dynamic-update-slice | bytes 786436 | tf_op jit(solution)/shard_map/dynamic_update_slice | solution.py:27
  315.9 33.9 %dynamic_update_slice.32 = f32[2,6,1,32,16,128]{5,3,4,1,2,0:T(8,128)} dynamic-update-slice(f32[2,6,1,32,16,128]{5,3,4,1,2,0:T(8,128)} %dynamic_update_slice.31, f32[2,6,1,32,16,16]{5,3,4,1,2,0:T(8,128)} %copy.72, s32[]{:T(128)} %constant.104.clone.1, s32[]{:T(128)} %constant.104.clone.1, s32[]{:T(128)} %constant.104.clone.1, s32[]{:T(128)} %constant.104.clone.1, s32[]{:T(128)} %constant.104.clone.1, ...) | dynamic-update-slice | bytes 786436 | tf_op jit(solution)/shard_map/dynamic_update_slice | solution.py:27
  353.1 33.9 %dynamic_update_slice.33 = f32[2,6,1,32,16,128]{5,3,4,1,2,0:T(8,128)} dynamic-update-slice(f32[2,6,1,32,16,128]{5,3,4,1,2,0:T(8,128)} %dynamic_update_slice.32, f32[2,6,1,32,16,16]{5,3,4,1,2,0:T(8,128)} %copy.74, s32[]{:T(128)} %constant.104.clone.1, s32[]{:T(128)} %constant.104.clone.1, s32[]{:T(128)} %constant.104.clone.1, s32[]{:T(128)} %constant.104.clone.1, s32[]{:T(128)} %constant.104.clone.1, ...) | dynamic-update-slice | bytes 786436 | tf_op jit(solution)/shard_map/dynamic_update_slice | solution.py:27
  390.3 33.9 %dynamic_update_slice.34 = f32[2,6,1,32,16,128]{5,3,4,1,2,0:T(8,128)} dynamic-update-slice(f32[2,6,1,32,16,128]{5,3,4,1,2,0:T(8,128)} %dynamic_update_slice.33, f32[2,6,1,32,16,16]{5,3,4,1,2,0:T(8,128)} %copy.76, s32[]{:T(128)} %constant.104.clone.1, s32[]{:T(128)} %constant.104.clone.1, s32[]{:T(128)} %constant.104.clone.1, s32[]{:T(128)} %constant.104.clone.1, s32[]{:T(128)} %constant.104.clone.1, ...) | dynamic-update-slice | bytes 786436 | tf_op jit(solution)/shard_map/dynamic_update_slice | solution.py:27
  427.5 33.9 %dynamic_update_slice.35 = f32[2,6,1,32,16,128]{5,3,4,1,2,0:T(8,128)} dynamic-update-slice(f32[2,6,1,32,16,128]{5,3,4,1,2,0:T(8,128)} %dynamic_update_slice.34, f32[2,6,1,32,16,16]{5,3,4,1,2,0:T(8,128)} %copy.78, s32[]{:T(128)} %constant.104.clone.1, s32[]{:T(128)} %constant.104.clone.1, s32[]{:T(128)} %constant.104.clone.1, s32[]{:T(128)} %constant.104.clone.1, s32[]{:T(128)} %constant.104.clone.1, ...) | dynamic-update-slice | bytes 786436 | tf_op jit(solution)/shard_map/dynamic_update_slice | solution.py:27
  464.7 33.9 %dynamic_update_slice.36 = f32[2,6,1,32,16,128]{5,3,4,1,2,0:T(8,128)} dynamic-update-slice(f32[2,6,1,32,16,128]{5,3,4,1,2,0:T(8,128)} %dynamic_update_slice.35, f32[2,6,1,32,16,16]{5,3,4,1,2,0:T(8,128)} %copy.80, s32[]{:T(128)} %constant.104.clone.1, s32[]{:T(128)} %constant.104.clone.1, s32[]{:T(128)} %constant.104.clone.1, s32[]{:T(128)} %constant.104.clone.1, s32[]{:T(128)} %constant.104.clone.1, ...) | dynamic-update-slice | bytes 786436 | tf_op jit(solution)/shard_map/dynamic_update_slice | solution.py:27
  501.9 33.9 %dynamic_update_slice.37 = f32[2,6,1,32,16,128]{5,3,4,1,2,0:T(8,128)} dynamic-update-slice(f32[2,6,1,32,16,128]{5,3,4,1,2,0:T(8,128)} %dynamic_update_slice.36, f32[2,6,1,32,16,16]{5,3,4,1,2,0:T(8,128)} %copy.82, s32[]{:T(128)} %constant.104.clone.1, s32[]{:T(128)} %constant.104.clone.1, s32[]{:T(128)} %constant.104.clone.1, s32[]{:T(128)} %constant.104.clone.1, s32[]{:T(128)} %constant.104.clone.1, ...) | dynamic-update-slice | bytes 786436 | tf_op jit(solution)/shard_map/dynamic_update_slice | solution.py:27
  539.1 34.3 %dynamic_update_slice.38 = f32[2,6,1,32,16,128]{5,3,4,1,2,0:T(8,128)} dynamic-update-slice(f32[2,6,1,32,16,128]{5,3,4,1,2,0:T(8,128)} %dynamic_update_slice.37, f32[2,6,1,32,16,16]{5,3,4,1,2,0:T(8,128)} %copy.84, s32[]{:T(128)} %constant.104.clone.1, s32[]{:T(128)} %constant.104.clone.1, s32[]{:T(128)} %constant.104.clone.1, s32[]{:T(128)} %constant.104.clone.1, s32[]{:T(128)} %constant.104.clone.1, ...) | dynamic-update-slice | bytes 786436 | tf_op jit(solution)/shard_map/dynamic_update_slice | solution.py:27
  584.0 11.4 %copy.85 = f32[2,6,1,16,128,32]{5,3,1,2,0,4:T(8,128)} copy(f32[2,6,1,16,128,32]{4,5,3,1,2,0:T(8,128)} %pad_maximum_fusion) | data formatting | bytes 6291456 | tf_op jit(solution)/shard_map/stack | solution.py:52
  595.4 9.3 reshape.562
  604.7 4.8 all-to-all-start.2
  612.5 34.2 %all-to-all-done.2 = f32[4,1,196608]{2,1,0:T(1,128)} async-done(((f32[4,1,196608]{2,1,0:T(1,128)}), f32[4,1,196608]{2,1,0:T(1,128)}, u32[]{:S(2)}, u32[]{:S(2)}) %all-to-all-start.2) | async-done | bytes 3145760 | tf_op jit(solution)/shard_map/all_to_all | solution.py:137
  646.7 11.8 %reduce.4 = f32[4,196608]{1,0:T(4,128)} reduce(f32[4,1,196608]{2,1,0:T(1,128)} %all-to-all-done.2, f32[]{:T(128)} %broadcast.808), dimensions={1}, to_apply=%all_to_all.39.reduce_sub_computation | reduce | bytes 6291460 | tf_op jit(solution)/shard_map/all_to_all | solution.py:137
  658.6 10.8 %reshape.563 = f32[128,2,1,6,16,32]{5,4,3,2,1,0:T(8,128)} reshape(f32[4,196608]{1,0:T(4,128)} %reduce.4) | data formatting | bytes 6291456
  669.3 16.4 %copy.104 = f32[2,6,1,16,4,32,32]{6,4,5,3,1,2,0:T(4,128)} copy(f32[2,6,1,16,4,32,32]{6,3,1,0,5,4,2:T(8,128)} %bitcast.273) | data formatting | bytes 6291456 | tf_op jit(solution)/shard_map/all_to_all | solution.py:137
  685.8 14.4 %fusion.212 = (f32[1,6,1,16,32,4,32]{6,5,4,3,1,2,0:T(4,128)}, f32[1,6,1,16,32,4,32]{6,5,4,3,1,2,0:T(4,128)}) fusion(f32[2,6,1,16,32,4,32]{6,5,4,3,1,2,0:T(4,128)} %bitcast.272), kind=kLoop, calls=%fused_computation.297 | loop fusion | bytes 6291456 | tf_op jit(solution)/shard_map/slice | solution.py:139
  700.2 6.0 reshape.548
  709.3 5.8 reshape.549
  721.0 165.9 %while.24 = (s32[]{:T(128)}, f32[9,65536]{1,0:T(8,128)}, f32[9,256]{1,0:T(8,128)S(1)}, f32[256]{0:T(256)S(1)}, f32[256,256]{1,0:T(8,128)S(1)}, /*index=5*/f32[25...) while((s32[]{:T(128)}, f32[9,65536]{1,0:T(8,128)}, ...), condition=%wide.region_3.4_spmd.clone, body=%wide.region_0.3_spmd.clone.sunk | while | flops 3422691328 | bytes 157343136 | solution.py:166
  727.0 3.9 convert_reduce_fusion.5
  731.0 4.3 fusion.272
  735.3 3.7 convolution_add_fusion.11
  747.7 3.9 convert_reduce_fusion.5
  751.7 4.3 fusion.272
  756.0 3.7 convolution_add_fusion.11
  768.4 3.9 convert_reduce_fusion.5
  772.4 4.3 fusion.272
  776.7 3.7 convolution_add_fusion.11
  789.1 3.9 convert_reduce_fusion.5
  793.1 4.3 fusion.272
  797.4 3.7 convolution_add_fusion.11
  809.8 3.9 convert_reduce_fusion.5
  813.8 4.4 fusion.272
  818.1 3.7 convolution_add_fusion.11
  830.5 3.9 convert_reduce_fusion.5
  834.5 4.4 fusion.272
  851.3 3.9 convert_reduce_fusion.5
  855.2 4.3 fusion.272
  859.6 3.7 convolution_add_fusion.11
  871.9 3.9 convert_reduce_fusion.5
  875.9 4.3 fusion.272
  880.2 3.7 convolution_add_fusion.11
  886.9 37.1 %all-reduce = (f32[9,256]{1,0:T(8,128)S(1)}, f32[256]{0:T(256)S(1)}, f32[256]{0:T(256)S(1)}, f32[256,6]{0,1:T(8,128)S(1)}) all-reduce(f32[9,256]{1,0:T(8,128)S(1)} %get-tuple-element.241, f32[256]{0:T(256)S(1)} %get-tuple-element.242, f32[256]{0:T(256)S(1)} %get-tuple-element.244, ...), channel_id=1, replica_groups=mesh['row'=8,'col'=4] {'row','col'}, use_global_device_ids=true, to_apply=%region_4.5 | all-reduce | flops 4352 | bytes 34816 | tf_op jit(solution)/shard_map/psum | solution.py:167
  931.0 125.9 %all-reduce.3.cloned.1.call-done = f32[256,256]{1,0:T(8,128)} async-done(((f32[256,256]{1,0:T(8,128)}), f32[256,256]{1,0:T(8,128)}) %all-reduce.3.cloned.1.call-update) | async-done | bytes 262160 | tf_op jit(solution)/shard_map/psum | solution.py:167
  (265 shorter events, 189.5 us)
Async XLA Ops:
  94.8 42.8 %all-to-all-start.1 = ((f32[8,1,49152]{2,1,0:T(1,128)}), f32[8,1,49152]{2,1,0:T(1,128)S(1)}, u32[]{:S(2)}, u32[]{:S(2)}) async-start(f32[8,1,49152]{2,1,0:T(1,128)} %reshape.560), calls=%async_computation.1 | async-start | bytes 3145728 | tf_op jit(solution)/shard_map/all_to_all | solution.py:104
  184.4 9.9 copy-start.9
  197.6 26.3 %collective-permute-start = (f32[2,6,1,32,16,16]{3,5,4,2,1,0:T(8,128)}, f32[2,6,1,32,16,16]{3,5,4,2,1,0:T(8,128)}, u32[]{:S(2)}, u32[]{:S(2)}) collective-permute-start(f32[2,6,1,32,16,16]{3,5,4,2,1,0:T(8,128)} %copy.71), channel_id=1, source_target_pairs={{0,4},{4,0},{8,12},{12,8},{16,20},{20,16},{24,28},{28,24},{1,5},{5... | collective-permute-start | bytes 1179656 | tf_op jit(solution)/shard_map/ppermute | solution.py:26
  201.0 86.9 %collective-permute-start.1 = (f32[2,6,1,32,16,16]{3,5,4,2,1,0:T(8,128)}, f32[2,6,1,32,16,16]{3,5,4,2,1,0:T(8,128)}, u32[]{:S(2)}, u32[]{:S(2)}) collective-permute-start(f32[2,6,1,32,16,16]{3,5,4,2,1,0:T(8,128)} %copy.73), channel_id=1, source_target_pairs={{0,8},{4,12},{8,0},{12,4},{16,24},{20,28},{24,16},{28,20},{1,9},{5... | collective-permute-start | bytes 1179656 | tf_op jit(solution)/shard_map/ppermute | solution.py:26
  213.0 174.0 %collective-permute-start.2 = (f32[2,6,1,32,16,16]{3,5,4,2,1,0:T(8,128)}, f32[2,6,1,32,16,16]{3,5,4,2,1,0:T(8,128)}, u32[]{:S(2)}, u32[]{:S(2)}) collective-permute-start(f32[2,6,1,32,16,16]{3,5,4,2,1,0:T(8,128)} %copy.75), channel_id=1, source_target_pairs={{0,12},{4,8},{8,4},{12,0},{16,28},{20,24},{24,20},{28,16},{1,13},{... | collective-permute-start | bytes 1179656 | tf_op jit(solution)/shard_map/ppermute | solution.py:26
  218.0 206.1 %collective-permute-start.3 = (f32[2,6,1,32,16,16]{3,5,4,2,1,0:T(8,128)}, f32[2,6,1,32,16,16]{3,5,4,2,1,0:T(8,128)}, u32[]{:S(2)}, u32[]{:S(2)}) collective-permute-start(f32[2,6,1,32,16,16]{3,5,4,2,1,0:T(8,128)} %copy.77), channel_id=1, source_target_pairs={{0,16},{4,20},{8,24},{12,28},{16,0},{20,4},{24,8},{28,12},{1,17},{... | collective-permute-start | bytes 1179656 | tf_op jit(solution)/shard_map/ppermute | solution.py:26
  218.2 243.2 %collective-permute-start.4 = (f32[2,6,1,32,16,16]{3,5,4,2,1,0:T(8,128)S(1)}, f32[2,6,1,32,16,16]{3,5,4,2,1,0:T(8,128)}, u32[]{:S(2)}, u32[]{:S(2)}) collective-permute-start(f32[2,6,1,32,16,16]{3,5,4,2,1,0:T(8,128)S(1)} %copy.79), channel_id=1, source_target_pairs={{0,20},{4,16},{8,28},{12,24},{16,4},{20,0},{24,12},{28,8},{1,21},{... | collective-permute-start | bytes 1179656 | tf_op jit(solution)/shard_map/ppermute | solution.py:26
  223.9 274.7 %collective-permute-start.5 = (f32[2,6,1,32,16,16]{3,5,4,2,1,0:T(8,128)}, f32[2,6,1,32,16,16]{3,5,4,2,1,0:T(8,128)}, u32[]{:S(2)}, u32[]{:S(2)}) collective-permute-start(f32[2,6,1,32,16,16]{3,5,4,2,1,0:T(8,128)} %copy.81), channel_id=1, source_target_pairs={{0,24},{4,28},{8,16},{12,20},{16,8},{20,12},{24,0},{28,4},{1,25},{... | collective-permute-start | bytes 1179656 | tf_op jit(solution)/shard_map/ppermute | solution.py:26
  287.9 247.9 %collective-permute-start.6 = (f32[2,6,1,32,16,16]{3,5,4,2,1,0:T(8,128)}, f32[2,6,1,32,16,16]{3,5,4,2,1,0:T(8,128)}, u32[]{:S(2)}, u32[]{:S(2)}) collective-permute-start(f32[2,6,1,32,16,16]{3,5,4,2,1,0:T(8,128)} %copy.83), channel_id=1, source_target_pairs={{0,28},{4,24},{8,20},{12,16},{16,12},{20,8},{24,4},{28,0},{1,29},{... | collective-permute-start | bytes 1179656 | tf_op jit(solution)/shard_map/ppermute | solution.py:26
  573.4 3.3 copy-start.8
  604.7 4.9 copy-start.11
  604.7 42.0 %all-to-all-start.2 = ((f32[4,1,196608]{2,1,0:T(1,128)}), f32[4,1,196608]{2,1,0:T(1,128)}, u32[]{:S(2)}, u32[]{:S(2)}) async-start(f32[4,1,196608]{2,1,0:T(1,128)} %reshape.562), calls=%async_computation.2 | async-start | bytes 6291456 | tf_op jit(solution)/shard_map/all_to_all | solution.py:137
  609.5 447.4 %all-reduce.3.cloned.1.call-start = ((), (), s32[]{:S(2)}) async-start(), calls=%async_computation.3 | async-start | bytes 524288 | tf_op jit(solution)/shard_map/psum | solution.py:167
  718.2 2.8 copy-start.12
  718.2 2.8 copy-start.13
  718.2 2.8 copy-start.14
  718.2 2.8 copy-start.15
  718.2 2.8 copy-start.16
  723.7 3.3 copy-start.3
  727.0 4.0 copy-start.5
  731.0 4.4 copy-start.4
  735.3 3.7 copy-start.2
  739.0 2.3 copy-start.7
  744.3 3.4 copy-start.3
  745.6 2.1 copy-start.6
  747.7 4.0 copy-start.5
  751.7 4.4 copy-start.4
  756.0 3.7 copy-start.2
  759.7 2.3 copy-start.7
  765.0 3.4 copy-start.3
  766.3 2.1 copy-start.6
  768.4 4.0 copy-start.5
  772.4 4.4 copy-start.4
  776.7 3.7 copy-start.2
  780.4 2.3 copy-start.7
  785.7 3.4 copy-start.3
  789.1 4.0 copy-start.5
  793.1 4.4 copy-start.4
  797.4 3.7 copy-start.2
  801.1 2.3 copy-start.7
  806.4 3.4 copy-start.3
  807.7 2.1 copy-start.6
  809.8 4.0 copy-start.5
  813.8 4.4 copy-start.4
  818.1 3.7 copy-start.2
  821.9 2.3 copy-start.7
  827.2 3.4 copy-start.3
  830.5 4.0 copy-start.5
  834.5 4.4 copy-start.4
  838.9 3.7 copy-start.2
  842.6 2.3 copy-start.7
  847.9 3.4 copy-start.3
  849.2 2.1 copy-start.6
  851.2 4.0 copy-start.5
  855.2 4.3 copy-start.4
  859.6 3.7 copy-start.2
  863.3 2.3 copy-start.7
  868.6 3.4 copy-start.3
  871.9 4.0 copy-start.5
  875.9 4.4 copy-start.4
  880.2 3.7 copy-start.2
  884.0 2.3 copy-start.7
  886.9 42.0 %copy-start.10 = (f32[256,256]{1,0:T(8,128)}, f32[256,256]{1,0:T(8,128)S(1)}, u32[]{:S(2)}) copy-start(f32[256,256]{1,0:T(8,128)S(1)} %get-tuple-element.243) | copy-start | bytes 786436
  925.8 132.8 %copy-start.1 = (f32[3,1,16,32,128]{4,3,2,1,0:T(8,128)S(1)}, f32[3,1,16,32,128]{4,3,2,1,0:T(8,128)}, u32[]{:S(2)}) copy-start(f32[3,1,16,32,128]{4,3,2,1,0:T(8,128)} %param.10) | copy-start | bytes 2359300
  (5 other events, 9.4 us)
Sparse Core Ops, SparseCore 0:
  930.6 126.2 all-reduce.2
